TPU v7x, 32 devices: a whole 2x2x4 slice. The times are simulated.
32 devices in a mesh: dp: 8 (over z, y), tensor: 4 (over x, core).
Axes of the slice: x: 2, y: 2, z: 4, core: 2. Of those that a mesh axis runs over, the one named last changes fastest.
Arguments:
- tokens: bfloat16 [16384, 768], P(('dp', 'tensor')), may hold values from -6 to 6
- lengths: int32 [8], P('dp'), may hold values from 512 to 2048, as said below
- arrival_slots: int32 [8, 2048], P('dp'), may hold values from 0 to 2047, each once within a row
- w_qkv: float32 [3, 768, 768], P(None, 'dp', 'tensor'), may hold values from -0.21875 to 0.21875
- w_out: float32 [768, 768], P('tensor', 'dp'), may hold values from -1.75 to 1.75
- w_up: float32 [768, 3072], P('dp', 'tensor'), may hold values from -0.21875 to 0.21875
- w_down: float32 [3072, 768], P('tensor', 'dp'), may hold values from -0.109375 to 0.109375
- w_proj: float32 [768, 128], P('dp'), may hold values from -0.21875 to 0.21875
- norm_gains: float32 [2, 768], P(None, 'dp'), may hold values from 0.1 to 1.9
- biases: float32 [6, 768], P(None, 'dp'), may hold values from -4 to 4
- up_bias: float32 [3072], P('dp'), may hold values from -4 to 4
- cotangent: bfloat16 [16384, 128], P(('dp', 'tensor')), may hold values from -6 to 6
Outputs:
- embeddings: float32 [16384, 128], P(('dp', 'tensor'))
- grad_tokens: float32 [16384, 768], P(('dp', 'tensor'))
- grad_qkv: float32 [3, 768, 768], P(None, 'dp', 'tensor')
- grad_out: float32 [768, 768], P('tensor', 'dp')
- grad_up: float32 [768, 3072], P('dp', 'tensor')
- grad_down: float32 [3072, 768], P('tensor', 'dp')
- grad_proj: float32 [768, 128], P('dp')
- grad_gains: float32 [2, 768], P(None, 'dp')
- grad_biases: float32 [6, 768], P(None, 'dp')
- grad_up_bias: float32 [3072], P('dp')
Inputs may be any that keep to these rules, and one draw needn't show every extreme that they name: `lengths`: some passage fills its whole slot of 2048 positions. `arrival_slots`: each row names every slot of its group once.
All inputs are finite; a program needn't handle non-finite values.
Results may differ from a plain program's by a relative error of at most 0.02.
Values may be sent and summed in bfloat16 or wider, within the bound.
A program may use at most 128 MiB of HBM per device.

v0:
```python
import jax
import jax.numpy as jnp
from jax import lax
from jax.sharding import PartitionSpec as P

HEAD_DIM = 64
SLOT = 2048
EPS_NORM = 1e-06
EPS_UNIT = 1e-06
NEG_FILL = -1e30


def norm_rows(values, gain, shift):
    center = values - jnp.mean(values, axis=-1, keepdims=True)
    spread = jnp.mean(center * center, axis=-1, keepdims=True)
    return center * lax.rsqrt(spread + EPS_NORM) * gain + shift


def gelu_exact(values):
    return jax.nn.gelu(values, approximate=False)


def contract_rows(left, right):
    return lax.dot_general(
        left, right, (((0,), (0,)), ((), ())), preferred_element_type=jnp.float32
    )


def times_transposed(left, right):
    return lax.dot_general(
        left, right, (((1,), (1,)), ((), ())), preferred_element_type=jnp.float32
    )


def attend(query_heads, key_heads, value_heads, key_mask, num_blocks, factor):

    def one_block(position):
        passage_idx = position // num_blocks
        block_idx = position % num_blocks
        query_block = query_heads[passage_idx, block_idx]
        scores = (
            jnp.einsum(
                "qhe,khe->hqk",
                query_block,
                key_heads[passage_idx],
                preferred_element_type=jnp.float32,
            )
            * factor
        )
        scores = jnp.where(key_mask[passage_idx][None, None, :], scores, NEG_FILL)
        row_top = jnp.max(scores, axis=-1, keepdims=True)
        shifted = jnp.exp(scores - row_top)
        row_total = jnp.sum(shifted, axis=-1, keepdims=True)
        soft_low = (shifted / row_total).astype(jnp.bfloat16)
        result = jnp.einsum(
            "hqk,khe->qhe", soft_low, value_heads[passage_idx], preferred_element_type=jnp.float32
        )
        return (result, (row_top + jnp.log(row_total))[..., 0])

    return lax.map(one_block, jnp.arange(query_heads.shape[0] * num_blocks))


def attend_back(
    query_heads, key_heads, value_heads, dcontext_heads, log_total, key_mask, num_blocks, factor
):

    def passage(passage_idx):
        key_rows = key_heads[passage_idx]
        value_rows = value_heads[passage_idx]
        mask_row = key_mask[passage_idx][None, None, :]

        def step(carry, block_idx):
            dkey_sum, dvalue_sum = carry
            query_block = query_heads[passage_idx, block_idx]
            dout_block = dcontext_heads[passage_idx, block_idx]
            total_block = log_total[passage_idx * num_blocks + block_idx]
            scores = (
                jnp.einsum(
                    "qhe,khe->hqk", query_block, key_rows, preferred_element_type=jnp.float32
                )
                * factor
            )
            scores = jnp.where(mask_row, scores, NEG_FILL)
            soft_probs = jnp.exp(scores - total_block[..., None])
            dvalue_sum = dvalue_sum + jnp.einsum(
                "hqk,qhe->khe",
                soft_probs.astype(jnp.bfloat16),
                dout_block,
                preferred_element_type=jnp.float32,
            )
            dsoft = jnp.einsum(
                "qhe,khe->hqk", dout_block, value_rows, preferred_element_type=jnp.float32
            )
            dscore = (
                soft_probs * (dsoft - jnp.sum(soft_probs * dsoft, axis=-1, keepdims=True))
            ).astype(jnp.bfloat16)
            dquery = (
                jnp.einsum("hqk,khe->qhe", dscore, key_rows, preferred_element_type=jnp.float32)
                * factor
            )
            dkey_sum = (
                dkey_sum
                + jnp.einsum(
                    "hqk,qhe->khe", dscore, query_block, preferred_element_type=jnp.float32
                )
                * factor
            )
            return ((dkey_sum, dvalue_sum), dquery)

        zero_grad = jnp.zeros(key_rows.shape, jnp.float32)
        (dkey_sum, dvalue_sum), dquery = lax.scan(
            step, (zero_grad, zero_grad), jnp.arange(num_blocks)
        )
        return (dquery, dkey_sum, dvalue_sum)

    return lax.map(passage, jnp.arange(key_heads.shape[0]))


def body(
    tokens,
    lengths,
    arrival_slots,
    w_qkv,
    w_out,
    w_up,
    w_down,
    w_proj,
    norm_gains,
    biases,
    up_bias,
    cotangent,
):
    tensor_size = lax.axis_size("tensor")
    tensor_pos = lax.axis_index("tensor")
    own_rows = tokens.shape[0]
    group_rows = own_rows * tensor_size
    passages = group_rows // SLOT
    block_rows = min(512, SLOT)
    num_blocks = SLOT // block_rows
    factor = HEAD_DIM ** (-0.5)
    slot_order = arrival_slots[0]
    gathered = (
        lax.all_gather(w_qkv.astype(jnp.bfloat16), "dp", axis=1, tiled=True),
        lax.all_gather(w_out.astype(jnp.bfloat16), "dp", axis=1, tiled=True),
        lax.all_gather(w_up.astype(jnp.bfloat16), "dp", axis=0, tiled=True),
        lax.all_gather(w_down.astype(jnp.bfloat16), "dp", axis=1, tiled=True),
        lax.all_gather(w_proj.astype(jnp.bfloat16), "dp", axis=0, tiled=True),
        lax.all_gather(norm_gains.astype(jnp.bfloat16), "dp", axis=1, tiled=True),
        lax.all_gather(biases.astype(jnp.bfloat16), "dp", axis=1, tiled=True),
        lax.all_gather(up_bias.astype(jnp.bfloat16), "dp", axis=0, tiled=True),
    )
    qkv_weight, out_weight, up_weight, down_weight, proj_weight, gain_low, bias_low, upbias_low = (
        gathered
    )
    width_local = qkv_weight.shape[2]
    hidden_local = up_weight.shape[1]
    heads_local = width_local // HEAD_DIM
    gain_full = gain_low.astype(jnp.float32)
    bias_full = bias_low.astype(jnp.float32)
    upbias_full = upbias_low.astype(jnp.float32)
    col_start = tensor_pos * width_local
    query_bias = lax.dynamic_slice_in_dim(bias_full[0], col_start, width_local)
    value_bias = lax.dynamic_slice_in_dim(bias_full[1], col_start, width_local)
    arrived = lax.all_gather(tokens, "tensor", axis=0, tiled=True)
    inverse = (
        jnp.zeros((group_rows,), jnp.int32)
        .at[slot_order]
        .set(jnp.arange(group_rows, dtype=jnp.int32))
    )
    slotted = jnp.take(arrived, inverse, axis=0)
    row_start = tensor_pos * own_rows
    resid_input = lax.dynamic_slice_in_dim(slotted, row_start, own_rows, 0).astype(jnp.float32)
    positions = row_start + jnp.arange(own_rows, dtype=jnp.int32)
    row_keep = (positions % SLOT < lengths[positions // SLOT]).astype(jnp.float32)
    key_mask = jnp.arange(SLOT, dtype=jnp.int32)[None, :] < lengths[:, None]
    qkv_bias = jnp.stack([query_bias, jnp.zeros_like(query_bias), value_bias])
    qkv_all = (
        jnp.einsum("gd,cde->cge", slotted, qkv_weight, preferred_element_type=jnp.float32)
        + qkv_bias[:, None, :]
    ).astype(jnp.bfloat16)
    block_shape = (passages, num_blocks, block_rows, heads_local, HEAD_DIM)
    slot_shape = (passages, SLOT, heads_local, HEAD_DIM)
    query_heads = qkv_all[0].reshape(block_shape)
    key_heads = qkv_all[1].reshape(slot_shape)
    value_heads = qkv_all[2].reshape(slot_shape)
    attended, log_total = attend(query_heads, key_heads, value_heads, key_mask, num_blocks, factor)
    context = attended.reshape(group_rows, width_local).astype(jnp.bfloat16)
    attn_part = lax.psum_scatter(
        jnp.dot(context, out_weight, preferred_element_type=jnp.float32).astype(jnp.bfloat16),
        "tensor",
        scatter_dimension=0,
        tiled=True,
    ).astype(jnp.float32)
    first_sum = resid_input + attn_part + bias_full[2]
    first_norm, back_first = jax.vjp(norm_rows, first_sum, gain_full[0], bias_full[3])
    first_low = first_norm.astype(jnp.bfloat16)
    mid_rows = lax.all_gather(first_low, "tensor", axis=0, tiled=True)
    upbias_own = lax.dynamic_slice_in_dim(upbias_full, tensor_pos * hidden_local, hidden_local)
    ffn_pre = jnp.dot(mid_rows, up_weight, preferred_element_type=jnp.float32) + upbias_own
    hidden = gelu_exact(ffn_pre).astype(jnp.bfloat16)
    ffn_part = lax.psum_scatter(
        jnp.dot(hidden, down_weight, preferred_element_type=jnp.float32).astype(jnp.bfloat16),
        "tensor",
        scatter_dimension=0,
        tiled=True,
    ).astype(jnp.float32)
    second_sum = first_norm + ffn_part + bias_full[4]
    second_norm, back_second = jax.vjp(norm_rows, second_sum, gain_full[1], bias_full[5])
    second_low = second_norm.astype(jnp.bfloat16)
    projected = jnp.dot(second_low, proj_weight, preferred_element_type=jnp.float32)

    def unit_rows(values):
        return (
            values
            * lax.rsqrt(jnp.sum(values * values, axis=-1, keepdims=True) + EPS_UNIT)
            * row_keep[:, None]
        )

    embeddings, back_unit = jax.vjp(unit_rows, projected)
    (dproj,) = back_unit(cotangent.astype(jnp.float32))
    dproj_low = dproj.astype(jnp.bfloat16)
    grad_proj = contract_rows(second_low, dproj_low)
    dsecond_norm = times_transposed(dproj_low, proj_weight)
    dsecond, grad_gain_two, grad_shift_two = back_second(dsecond_norm)
    dsecond_low = dsecond.astype(jnp.bfloat16)
    dsecond_rows = lax.all_gather(dsecond_low, "tensor", axis=0, tiled=True)
    dhidden = times_transposed(dsecond_rows, down_weight)
    grad_down = contract_rows(hidden, dsecond_rows)
    (dpre,) = jax.vjp(gelu_exact, ffn_pre)[1](dhidden)
    dpre_low = dpre.astype(jnp.bfloat16)
    grad_upbias = lax.dynamic_update_slice_in_dim(
        jnp.zeros(upbias_full.shape, jnp.float32),
        jnp.sum(dpre_low.astype(jnp.float32), axis=0),
        tensor_pos * hidden_local,
        0,
    )
    grad_up = contract_rows(mid_rows, dpre_low)
    dfirst_norm = lax.psum_scatter(
        times_transposed(dpre_low, up_weight).astype(jnp.bfloat16),
        "tensor",
        scatter_dimension=0,
        tiled=True,
    ).astype(jnp.float32)
    dfirst, grad_gain_one, grad_shift_one = back_first(dfirst_norm + dsecond)
    dfirst_low = dfirst.astype(jnp.bfloat16)
    dfirst_rows = lax.all_gather(dfirst_low, "tensor", axis=0, tiled=True)
    dcontext = times_transposed(dfirst_rows, out_weight).astype(jnp.bfloat16)
    grad_out = contract_rows(context, dfirst_rows)
    dquery, dkey, dvalue = attend_back(
        query_heads,
        key_heads,
        value_heads,
        dcontext.reshape(block_shape),
        log_total,
        key_mask,
        num_blocks,
        factor,
    )
    dqkv = jnp.stack(
        [
            dquery.reshape(group_rows, width_local),
            dkey.reshape(group_rows, width_local),
            dvalue.reshape(group_rows, width_local),
        ]
    ).astype(jnp.bfloat16)
    grad_qkv = jnp.einsum("gd,cge->cde", slotted, dqkv, preferred_element_type=jnp.float32)
    column_sums = jnp.sum(dqkv.astype(jnp.float32), axis=1)
    resid_full = lax.dynamic_update_slice_in_dim(
        jnp.zeros((group_rows, dfirst.shape[1]), jnp.float32), dfirst, row_start, 0
    )
    chosen = jnp.take(dqkv, slot_order, axis=1)
    through = jnp.einsum("cge,cde->gd", chosen, qkv_weight, preferred_element_type=jnp.float32)
    grad_tokens = lax.psum_scatter(
        (through + jnp.take(resid_full, slot_order, axis=0)).astype(jnp.bfloat16),
        "tensor",
        scatter_dimension=0,
        tiled=True,
    ).astype(jnp.float32)
    zero_row = jnp.zeros((bias_full.shape[1],), jnp.float32)
    grad_biases = jnp.stack(
        [
            lax.dynamic_update_slice_in_dim(zero_row, column_sums[0], col_start, 0),
            lax.dynamic_update_slice_in_dim(zero_row, column_sums[2], col_start, 0),
            jnp.sum(dfirst, axis=0),
            grad_shift_one,
            jnp.sum(dsecond, axis=0),
            grad_shift_two,
        ]
    )
    grad_gains = jnp.stack([grad_gain_one, grad_gain_two])
    grad_proj, grad_gains, grad_biases, grad_upbias = (
        lax.psum(grad_proj.astype(jnp.bfloat16), "tensor").astype(jnp.float32),
        lax.psum(grad_gains.astype(jnp.bfloat16), "tensor").astype(jnp.float32),
        lax.psum(grad_biases.astype(jnp.bfloat16), "tensor").astype(jnp.float32),
        lax.psum(grad_upbias.astype(jnp.bfloat16), "tensor").astype(jnp.float32),
    )
    summed = (
        lax.psum_scatter(grad_qkv, "dp", scatter_dimension=1, tiled=True),
        lax.psum_scatter(grad_out, "dp", scatter_dimension=1, tiled=True),
        lax.psum_scatter(grad_up, "dp", scatter_dimension=0, tiled=True),
        lax.psum_scatter(grad_down, "dp", scatter_dimension=1, tiled=True),
        lax.psum_scatter(grad_proj, "dp", scatter_dimension=0, tiled=True),
        lax.psum_scatter(grad_gains, "dp", scatter_dimension=1, tiled=True),
        lax.psum_scatter(grad_biases, "dp", scatter_dimension=1, tiled=True),
        lax.psum_scatter(grad_upbias, "dp", scatter_dimension=0, tiled=True),
    )
    return (
        embeddings,
        grad_tokens,
        summed[0],
        summed[1],
        summed[2],
        summed[3],
        summed[4],
        summed[5],
        summed[6],
        summed[7],
    )


def solution(mesh):
    return jax.shard_map(
        body,
        mesh=mesh,
        in_specs=(
            P(("dp", "tensor"), None),
            P("dp"),
            P("dp", None),
            P(None, "dp", "tensor"),
            P("tensor", "dp"),
            P("dp", "tensor"),
            P("tensor", "dp"),
            P("dp", None),
            P(None, "dp"),
            P(None, "dp"),
            P("dp"),
            P(("dp", "tensor"), None),
        ),
        out_specs=(
            P(("dp", "tensor"), None),
            P(("dp", "tensor"), None),
            P(None, "dp", "tensor"),
            P("tensor", "dp"),
            P("dp", "tensor"),
            P("tensor", "dp"),
            P("dp", None),
            P(None, "dp"),
            P(None, "dp"),
            P("dp"),
        ),
        check_vma=False,
    )
```

profile of v0, /device:TPU:0, one launch (start us, length us, event | category | flops | bytes accessed | tf_op | source)
XLA Modules:
  0.0 1148.0 jit_solution(114364910664673060)
XLA Ops:
  9.5 27.9 %all-gather = bf16[8,96,6]{1,2,0:T(8,128)(2,1)S(1)} all-gather(bf16[1,96,6]{1,2,0:T(8,128)(2,1)S(1)} %convert_bitcast_fusion), channel_id=1, replica_groups=mesh['dp'=8,'tensor'=4] {'dp'}, dimensions={0}, use_global_device_ids=true | all-gather | bytes 10368 | tf_op jit(solution)/shard_map/all_gather | solution.py:149
  39.6 36.3 %all_gather.37 = bf16[3,768,192]{2,0,1:T(4,128)(2,1)S(1)} all-gather(bf16[3,96,192]{2,0,1:T(4,128)(2,1)S(1)} %copy.61), channel_id=1, replica_groups=mesh['dp'=8,'tensor'=4] {'dp'}, dimensions={1}, use_global_device_ids=true | all-gather | bytes 995328 | tf_op jit(solution)/shard_map/all_gather | solution.py:143
  77.0 8.0 scatter_custom_fusion
  85.7 31.1 %all_gather.39 = bf16[192,768]{0,1:T(8,128)(2,1)S(1)} all-gather(bf16[192,96]{0,1:T(8,128)(2,1)S(1)} %copy.66), channel_id=1, replica_groups=mesh['dp'=8,'tensor'=4] {'dp'}, dimensions={1}, use_global_device_ids=true | all-gather | bytes 331776 | tf_op jit(solution)/shard_map/all_gather | solution.py:144
  117.0 12.4 %gather_fusion = bf16[2048,768]{1,0:T(8,128)(2,1)} fusion(bf16[2048,768]{1,0:T(8,128)(2,1)} %all-gather.10.cloned.1.call-done, s32[2048]{0:T(1024)S(1)} %fusion.65), kind=kCustom, calls=%fused_computation | custom fusion | bytes 6299648 | tf_op jit(solution)/shard_map/jit(_take)/gather | solution.py:170
  134.9 49.4 %while.44 = (s32[]{:T(128)}, bf16[4,512,3,64]{1,3,2,0:T(8,128)(2,1)S(1)}, f32[4,3,512]{2,1,0:T(4,128)}, s32[4]{0:T(128)S(1)}, bf16[1,4,512,3,64]{2,4,3,1,0:T(8,1...) while((s32[]{:T(128)}, ...), condition=%wide.region_4.5_spmd.clone, body=%wide.region_1.4_spmd.clone.sunk | while | flops 843055616 | bytes 39975208 | solution.py:60
  142.9 3.7 fusion.136
  152.5 2.8 fusion.135
  155.3 3.7 fusion.136
  167.6 3.7 fusion.136
  179.9 3.7 fusion.136
  189.5 18.1 %all-gather.1 = bf16[8,96,2]{1,2,0:T(2,128)(2,1)S(1)} all-gather(bf16[1,96,2]{1,2,0:T(2,128)(2,1)S(1)} %convert_bitcast_fusion.1), channel_id=1, replica_groups=mesh['dp'=8,'tensor'=4] {'dp'}, dimensions={0}, use_global_device_ids=true | all-gather | bytes 3456 | tf_op jit(solution)/shard_map/all_gather | solution.py:148
  207.7 16.3 %reduce-scatter.20.cloned.1.call-done = bf16[512,768]{1,0:T(8,128)(2,1)} async-done(((bf16[2048,768]{1,0:T(8,128)(2,1)}), bf16[512,768]{1,0:T(8,128)(2,1)}) %reduce-scatter.20.cloned.1.call-update) | async-done | bytes 786448 | tf_op jit(solution)/shard_map/reduce_scatter | solution.py:188
  231.1 26.3 %all-gather.2 = bf16[8,1,384]{2,1,0:T(2,128)(2,1)S(1)} all-gather(bf16[1,1,384]{2,1,0:T(2,128)(2,1)S(1)} %reshape.272), channel_id=1, replica_groups=mesh['dp'=8,'tensor'=4] {'dp'}, dimensions={0}, use_global_device_ids=true | all-gather | bytes 6912 | tf_op jit(solution)/shard_map/all_gather | solution.py:150
  259.3 19.0 %multiply_convert_fusion.1 = (bf16[2048,768]{1,0:T(8,128)(2,1)}, f32[2048,768]{1,0:T(8,128)}, f32[2048,768]{1,0:T(8,128)}) fusion(f32[768]{0:T(1024)S(1)} %dynamic_slice.71, bf16[2048,768]{1,0:T(8,128)(2,1)} %all-gather.12.cloned.1.call-done, bf16[768,768]{1,0:T(8,128)(2,1)} %all-gather.14.cloned.1.call-done), kind=kOutput, calls=%fused_computation.62 | convolution fusion | flops 2519728128 | bytes 20057088 | tf_op jit(solution)/shard_map/dot_general | solution.py:199
  278.3 25.1 %all-gather.16.cloned.1.call-done = bf16[768,768]{0,1:T(8,128)(2,1)} async-done(((bf16[768,96]{0,1:T(8,128)(2,1)}), bf16[768,768]{0,1:T(8,128)(2,1)}) %all-gather.16.cloned.1.call-update) | async-done | bytes 1179664 | tf_op jit(solution)/shard_map/all_gather | solution.py:146
  303.4 6.6 convolution_convert_fusion.1
  311.0 30.6 %all_gather.45 = bf16[768,128]{1,0:T(8,128)(2,1)S(1)} all-gather(bf16[96,128]{1,0:T(8,128)(2,1)S(1)} %convert_element_type.175), channel_id=1, replica_groups=mesh['dp'=8,'tensor'=4] {'dp'}, dimensions={0}, use_global_device_ids=true | all-gather | bytes 221184 | tf_op jit(solution)/shard_map/all_gather | solution.py:147
  341.7 4.5 reduce-scatter.22.cloned.1.call-done
  354.9 28.2 %all-gather.18.cloned.1.call-done = bf16[2048,768]{1,0:T(8,128)(2,1)} async-done(((bf16[512,768]{1,0:T(8,128)(2,1)}), bf16[2048,768]{1,0:T(8,128)(2,1)}) %all-gather.18.cloned.1.call-update) | async-done | bytes 3145744 | tf_op jit(solution)/shard_map/all_gather | solution.py:226
  383.1 11.1 convert_reduce_fusion
  395.9 4.0 convolution_convert_fusion
  400.0 37.8 %reduce-scatter.24.cloned.1.call-done = bf16[512,768]{1,0:T(8,128)(2,1)} async-done(((bf16[2048,768]{1,0:T(8,128)(2,1)}), bf16[512,768]{1,0:T(8,128)(2,1)}) %reduce-scatter.24.cloned.1.call-update) | async-done | bytes 786448 | tf_op jit(solution)/shard_map/reduce_scatter | solution.py:238
  437.8 3.6 multiply_reduce_fusion.2
  444.2 3.0 broadcast.326
  457.9 19.7 %all-gather.20.cloned.1.call-done = bf16[2048,768]{1,0:T(8,128)(2,1)} async-done(((bf16[512,768]{1,0:T(8,128)(2,1)}), bf16[2048,768]{1,0:T(8,128)(2,1)}) %all-gather.20.cloned.1.call-update) | async-done | bytes 3145744 | tf_op jit(solution)/shard_map/all_gather | solution.py:246
  477.6 4.0 convolution_convert_fusion.3
  481.6 3.0 reshape.230
  487.7 119.7 %while.45 = (s32[]{:T(128)}, f32[2048,3,64]{0,2,1:T(8,128)S(1)}, f32[2048,3,64]{0,2,1:T(8,128)}, bf16[4,512,3,64]{1,3,2,0:T(8,128)(2,1)}, s32[4]{0:T(128)S(1)}, ...) while((s32[]{:T(128)}, f32[2048,3,64]{0,2,1:T(8,128)S(1)}, ...), condition=%wide.region_20.21_spmd.clone, body=%wide.region_18.20_spmd.clone.sunk | while | flops 2062516736 | bytes 129419512 | solution.py:111
  494.4 4.9 fusion.148
  499.3 4.8 multiply_reduce_fusion.10
  504.2 5.0 multiply_convert_fusion.3
  509.1 5.7 fusion.149
  523.8 5.5 fusion.148
  529.3 4.8 multiply_reduce_fusion.10
  534.2 5.0 multiply_convert_fusion.3
  539.2 5.6 fusion.149
  553.8 5.5 fusion.148
  559.4 4.8 multiply_reduce_fusion.10
  564.2 5.0 multiply_convert_fusion.3
  569.2 5.6 fusion.149
  583.9 5.5 fusion.148
  589.4 4.8 multiply_reduce_fusion.10
  594.3 5.0 multiply_convert_fusion.3
  599.2 5.6 fusion.149
  613.8 10.6 all-reduce.1
  626.4 4.1 convolution_bitcast_fusion
  630.5 4.6 fusion.58
  635.2 2.9 copy.77
  638.1 4.7 reshape.281
  642.9 13.4 %gather_fusion.2 = f32[2048,768]{1,0:T(8,128)} fusion(f32[2048,768]{1,0:T(8,128)} %get-tuple-element.574, s32[2048]{0:T(1024)S(1)} %broadcast_clamp_fusion), kind=kCustom, calls=%fused_computation.2 | custom fusion | bytes 12591104 | tf_op jit(solution)/shard_map/jit(_take)/gather | solution.py:274
  656.4 7.0 copy.72
  663.3 18.9 %gather_fusion.1 = bf16[2048,3,192]{2,1,0:T(4,128)(2,1)} fusion(bf16[3,2048,192]{2,0,1:T(4,128)(2,1)} %copy.72, s32[2048]{0:T(1024)S(1)} %broadcast_clamp_fusion), kind=kCustom, calls=%fused_computation.1 | custom fusion | bytes 4726784 | tf_op jit(solution)/shard_map/jit(_take)/gather | solution.py:271
  682.2 9.7 select_bitcast_fusion
  691.9 6.2 fusion.48
  700.3 7.0 fusion.81
  707.3 6.9 fusion.82
  716.4 37.2 %all-reduce = f32[3072]{0:T(1024)S(1)} all-reduce(bf16[3072]{0:T(1024)(128)(2,1)S(1)} %get-tuple-element.552), channel_id=13, replica_groups=mesh['dp'=8,'tensor'=4] {'dp'}, use_global_device_ids=true, to_apply=%region_41.42.clone | all-reduce | flops 3072 | bytes 18432
  757.2 62.2 %reduce-scatter.36.cloned.1.call-done = f32[96,192]{1,0:T(8,128)} async-done(((f32[768,192]{1,0:T(8,128)}), f32[96,192]{1,0:T(8,128)}) %reduce-scatter.36.cloned.1.call-update) | async-done | bytes 73744
  821.0 67.9 %reduce-scatter.34.cloned.1.call-done = f32[96,576]{1,0:T(8,128)} async-done(((f32[768,576]{1,0:T(8,128)}), f32[96,576]{1,0:T(8,128)}) %reduce-scatter.34.cloned.1.call-update) | async-done | bytes 221200
  890.8 37.6 %reduce-scatter.26.cloned.1.call-done = bf16[512,768]{1,0:T(8,128)(2,1)} async-done(((bf16[2048,768]{1,0:T(8,128)(2,1)}), bf16[512,768]{1,0:T(8,128)(2,1)}) %reduce-scatter.26.cloned.1.call-update) | async-done | bytes 786448 | tf_op jit(solution)/shard_map/reduce_scatter | solution.py:273
  930.8 63.5 %reduce-scatter.32.cloned.1.call-done = f32[96,128]{1,0:T(8,128)} async-done(((f32[768,128]{1,0:T(8,128)}), f32[96,128]{1,0:T(8,128)}) %reduce-scatter.32.cloned.1.call-update) | async-done | bytes 49168 | tf_op jit(solution)/shard_map/reduce_scatter | solution.py:302
  994.4 72.9 %reduce-scatter.28.cloned.1.call-done = f32[96,768]{1,0:T(8,128)} async-done(((f32[768,768]{1,0:T(8,128)}), f32[96,768]{1,0:T(8,128)}) %reduce-scatter.28.cloned.1.call-update) | async-done | bytes 294928 | tf_op jit(solution)/shard_map/reduce_scatter | solution.py:300
  1067.3 73.1 %reduce-scatter.30.cloned.1.call-done = f32[768,96]{0,1:T(8,128)} async-done(((f32[768,768]{0,1:T(8,128)}), f32[768,96]{0,1:T(8,128)}) %reduce-scatter.30.cloned.1.call-update) | async-done | bytes 294928 | tf_op jit(solution)/shard_map/reduce_scatter | solution.py:301
  (273 shorter events, 125.8 us)
Async XLA Ops:
  8.0 68.9 %copy-start.19 = (s32[1,2048]{1,0:T(1,128)S(1)}, s32[1,2048]{1,0:T(1,128)}, u32[]{:S(2)}) copy-start(s32[1,2048]{1,0:T(1,128)} %param.18) | copy-start | bytes 24580
  8.0 109.0 %all-gather.10.cloned.1.call-start = ((), (), s32[]{:S(2)}) async-start(), calls=%async_computation.11 | async-start | bytes 3932160 | tf_op jit(solution)/shard_map/all_gather | solution.py:164
  8.8 215.3 %reduce-scatter.20.cloned.1.call-start = ((), (), s32[]{:S(2)}) async-start(), calls=%async_computation.12 | async-start | bytes 3932160 | tf_op jit(solution)/shard_map/reduce_scatter | solution.py:188
  76.8 54.7 %copy-start.12 = (bf16[3,768,192]{1,2,0:T(8,128)(2,1)}, bf16[3,768,192]{1,2,0:T(8,128)(2,1)S(1)}, u32[]{:S(2)}) copy-start(bf16[3,768,192]{1,2,0:T(8,128)(2,1)S(1)} %copy.62) | copy-start | bytes 2654212
  76.9 52.4 %copy-start.21 = (s32[2048,1]{0,1:T(1,128)}, s32[2048,1]{0,1:T(1,128)S(1)}, u32[]{:S(2)}) copy-start(s32[2048,1]{0,1:T(1,128)S(1)} %compare_select_fusion) | copy-start | bytes 24580
  131.5 2.1 copy-start.4
  184.3 3.5 copy-start.5
  185.1 2.7 copy-start.7
  185.1 4.4 copy-start.39
  187.8 1.0 copy-start.14
  187.8 69.7 %all-gather.14.cloned.1.call-start = ((), (), s32[]{:S(2)}) async-start(), calls=%async_computation.14 | async-start | bytes 1327104 | tf_op jit(solution)/shard_map/all_gather | solution.py:145
  189.4 69.9 %all-gather.12.cloned.1.call-start = ((), (), s32[]{:S(2)}) async-start(), calls=%async_computation.13 | async-start | bytes 3932160 | tf_op jit(solution)/shard_map/all_gather | solution.py:197
  224.0 3.6 copy-start.1
  224.0 6.2 copy-start.15
  224.0 7.0 copy-start.37
  227.7 3.4 copy-start.26
  230.2 73.2 %all-gather.16.cloned.1.call-start = ((), (), s32[]{:S(2)}) async-start(), calls=%async_computation.15 | async-start | bytes 1327104 | tf_op jit(solution)/shard_map/all_gather | solution.py:146
  231.0 115.2 %reduce-scatter.22.cloned.1.call-start = ((), (), s32[]{:S(2)}) async-start(), calls=%async_computation.16 | async-start | bytes 3932160 | tf_op jit(solution)/shard_map/reduce_scatter | solution.py:201
  257.5 20.9 %copy-start.35 = (f32[768]{0:T(1024)}, f32[768]{0:T(1024)S(1)}, u32[]{:S(2)}) copy-start(f32[768]{0:T(1024)S(1)} %dynamic_slice.71) | copy-start | bytes 9220
  310.0 0.8 copy-start.17
  310.0 0.9 copy-start.16
  310.0 36.2 %copy-start.18 = (f32[768]{0:T(1024)S(1)}, f32[768]{0:T(1024)}, u32[]{:S(2)}) copy-start(f32[768]{0:T(1024)} %get-tuple-element.508) | copy-start | bytes 9220
  310.0 36.2 %copy-start.28 = (f32[768]{0:T(1024)S(1)}, f32[768]{0:T(1024)}, u32[]{:S(2)}) copy-start(f32[768]{0:T(1024)} %get-tuple-element.507) | copy-start | bytes 9220
  310.0 38.7 %copy-start.27 = (f32[768]{0:T(1024)S(1)}, f32[768]{0:T(1024)}, u32[]{:S(2)}) copy-start(f32[768]{0:T(1024)} %get-tuple-element.506) | copy-start | bytes 9220
  310.0 73.1 %all-gather.18.cloned.1.call-start = ((), (), s32[]{:S(2)}) async-start(), calls=%async_computation.17 | async-start | bytes 3932160 | tf_op jit(solution)/shard_map/all_gather | solution.py:226
  349.0 2.5 copy-start.6
  350.2 2.0 copy-start.10
  351.6 31.6 %copy-start.36 = (f32[768]{0:T(1024)S(1)}, f32[768]{0:T(1024)}, u32[]{:S(2)}) copy-start(f32[768]{0:T(1024)} %copy-done.35) | copy-start | bytes 9220
  352.2 1.1 copy-start.2
  352.2 42.0 %copy-start.23 = (f32[512]{0:T(512)}, f32[512]{0:T(512)S(1)}, u32[]{:S(2)}) copy-start(f32[512]{0:T(512)S(1)} %negate_multiply_fusion.2) | copy-start | bytes 6148
  354.5 83.3 %reduce-scatter.24.cloned.1.call-start = ((), (), s32[]{:S(2)}) async-start(), calls=%async_computation.18 | async-start | bytes 3932160 | tf_op jit(solution)/shard_map/reduce_scatter | solution.py:238
  383.1 12.8 %copy-start.38 = (bf16[768,768]{1,0:T(8,128)(2,1)S(1)}, bf16[768,768]{1,0:T(8,128)(2,1)}, u32[]{:S(2)}) copy-start(bf16[768,768]{1,0:T(8,128)(2,1)} %all-gather.14.cloned.1.call-done) | copy-start | bytes 3538948
  394.3 1.6 copy-start.41
  399.9 77.7 %all-gather.20.cloned.1.call-start = ((), (), s32[]{:S(2)}) async-start(), calls=%async_computation.19 | async-start | bytes 3932160 | tf_op jit(solution)/shard_map/all_gather | solution.py:246
  437.8 4.3 copy-start.3
  437.8 4.3 copy-start.9
  447.2 2.4 copy-start.34
  448.9 249.3 %all-reduce.4.cloned.1.call-start = ((), (), s32[]{:S(2)}) async-start(), calls=%async_computation.23 | async-start | bytes 393216 | tf_op jit(solution)/shard_map/psum | solution.py:292
  452.5 301.7 %reduce-scatter.38.cloned.1.call-start = ((), (), s32[]{:S(2)}) async-start(), calls=%async_computation.27 | async-start | bytes 442368
  453.6 33.1 %copy-start.24 = (bf16[3072]{0:T(1024)(128)(2,1)}, bf16[3072]{0:T(1024)(128)(2,1)S(1)}, u32[]{:S(2)}) copy-start(bf16[3072]{0:T(1024)(128)(2,1)S(1)} %dynamic_update_slice.46) | copy-start | bytes 18436
  509.1 5.7 copy-start
  539.2 5.6 copy-start
  569.2 5.6 copy-start
  599.2 5.6 copy-start
  609.9 3.8 copy-start.30
  609.9 3.8 copy-start.31
  609.9 3.8 copy-start.32
  609.9 3.8 copy-start.33
  609.9 3.8 copy-start.25
  609.9 3.8 copy-start.29
  611.4 14.9 %copy-start.8 = (bf16[24,8,4,512]{3,1,2,0:T(8,128)(2,1)S(1)}, bf16[24,8,4,512]{3,1,2,0:T(8,128)(2,1)}, u32[]{:S(2)}) copy-start(bf16[24,8,4,512]{3,1,2,0:T(8,128)(2,1)} %copy-done.7) | copy-start | bytes 2359300
  625.3 130.4 %reduce-scatter.40.cloned.1.call-start = ((), (), s32[]{:S(2)}) async-start(), calls=%async_computation.28 | async-start | bytes 442368
  626.3 193.1 %reduce-scatter.36.cloned.1.call-start = ((), (), s32[]{:S(2)}) async-start(), calls=%async_computation.26 | async-start | bytes 884736
  630.5 258.4 %reduce-scatter.34.cloned.1.call-start = ((), (), s32[]{:S(2)}) async-start(), calls=%async_computation.25 | async-start | bytes 2211840
  638.1 4.8 copy-start.20
  638.1 4.8 copy-start.22
  642.8 285.6 %reduce-scatter.26.cloned.1.call-start = ((), (), s32[]{:S(2)}) async-start(), calls=%async_computation.20 | async-start | bytes 3932160 | tf_op jit(solution)/shard_map/reduce_scatter | solution.py:273
  682.2 9.7 copy-start.13
  698.2 296.2 %reduce-scatter.32.cloned.1.call-start = ((), (), s32[]{:S(2)}) async-start(), calls=%async_computation.24 | async-start | bytes 442368 | tf_op jit(solution)/shard_map/reduce_scatter | solution.py:302
  700.0 367.3 %reduce-scatter.28.cloned.1.call-start = ((), (), s32[]{:S(2)}) async-start(), calls=%async_computation.21 | async-start | bytes 2654208 | tf_op jit(solution)/shard_map/reduce_scatter | solution.py:300
  707.3 7.1 copy-start.40
  707.3 8.3 copy-start.11
  707.3 433.1 %reduce-scatter.30.cloned.1.call-start = ((), (), s32[]{:S(2)}) async-start(), calls=%async_computation.22 | async-start | bytes 2654208 | tf_op jit(solution)/shard_map/reduce_scatter | solution.py:301
Sparse Core Ops, SparseCore 0:
  10.4 31.2 all-gather.9
  187.9 36.0 reduce-scatter.19
  354.6 28.5 all-gather.17
  449.0 28.4 all-gather.19
  480.3 31.9 all-reduce.3
Sparse Core Ops, SparseCore 1:
  191.0 39.5 all-gather.13
  232.6 26.7 all-gather.11
  262.0 41.4 all-gather.15
  310.1 36.0 reduce-scatter.21
  400.0 37.7 reduce-scatter.23
  625.4 63.2 reduce-scatter.37
  691.8 61.3 reduce-scatter.39
  756.9 62.4 reduce-scatter.35
  822.7 66.2 reduce-scatter.33
  891.5 36.9 reduce-scatter.25
  932.2 62.1 reduce-scatter.31
  998.5 68.8 reduce-scatter.27
  1071.2 69.1 reduce-scatter.29
where the time goes:
time: 1150 us
  waiting for transfers between devices  512 us (45%)
  blocking collectives  218 us (19%)
  matrix products  189 us (16%)
  local copies, waits for them, and re-layouts  112 us (10%)
  other arithmetic  81.9 us (7%)
  between operations  18 us (2%)
  loops' own time  16 us (1%)
    unnamed x22, waiting for transfers between devices  131 us
    reduce_scatter x1, waiting for transfers between devices, body(): lax.psum_scatter(grad_down, 'dp', scatter_dimension=1, tiled=True)  73.1 us
    reduce_scatter x1, waiting for transfers between devices, body(): lax.psum_scatter(grad_up, 'dp', scatter_dimension=0, tiled=True)  72.9 us
    reduce_scatter x1, waiting for transfers between devices, body(): lax.psum_scatter(grad_proj, 'dp', scatter_dimension=0, tiled=True)  63.5 us
    reduce_scatter x1, waiting for transfers between devices, body(): lax.psum_scatter(times_transposed(dpre_low, up_weight).astype(jnp.bfloat1...  37.8 us
    reduce_scatter x1, waiting for transfers between devices, body(): lax.psum_scatter((through + jnp.take(resid_full, slot_order, axis=0)).ast...  37.6 us
    unnamed x1, blocking collectives  37.2 us
    all_gather x1, blocking collectives, body(): lax.all_gather(w_qkv.astype(jnp.bfloat16), 'dp', axis=1, tiled=True)  36.3 us
  transfers between devices with their start and end apart: 18, of which 13 were waited for; matrix products, arithmetic and copies ran while one was open for 24% of the time, Pallas kernels for 0%

commit v1 on v0

--- a/solution.py
+++ b/solution.py
@@ -223,7 +223,15 @@
     dsecond_norm = times_transposed(dproj_low, proj_weight)
     dsecond, grad_gain_two, grad_shift_two = back_second(dsecond_norm)
     dsecond_low = dsecond.astype(jnp.bfloat16)
-    dsecond_rows = lax.all_gather(dsecond_low, "tensor", axis=0, tiled=True)
+    ways, here, lap = (lax.axis_size("tensor"), lax.axis_index("tensor"), dsecond_low.shape[0])
+    line, have = (dsecond_low, 1)
+    while have < ways:
+        line = jnp.concatenate(
+            [line, lax.ppermute(line, "tensor", [(d, (d - have) % ways) for d in range(ways)])],
+            axis=0,
+        )
+        have = 2 * have
+    dsecond_rows = jnp.roll(line, here * lap, axis=0)
     dhidden = times_transposed(dsecond_rows, down_weight)
     grad_down = contract_rows(hidden, dsecond_rows)
     (dpre,) = jax.vjp(gelu_exact, ffn_pre)[1](dhidden)

time: 1150 us -> 1180 us (1.026)
  waiting for transfers between devices: 512 us -> 529 us
    ppermute x0 -> x2, waiting for transfers between devices: none -> 44.4 us  [body(): lax.ppermute(line, 'tensor', [(d, (d - have) % ways) for d in range(ways)])]
    all_gather x1 -> x0, waiting for transfers between devices: 28.2 us -> none  [body(): dsecond_rows = lax.all_gather(dsecond_low, 'tensor', axis=0, tiled=True)]
    unnamed x100 -> x110, local copies, waits for them, and re-layouts: 25.4 us -> 29.7 us
    unnamed x22 -> x21, waiting for transfers between devices: 131 us -> 131 us
  transfers between devices with their start and end apart: 18 -> 19, of which waited for: 13 -> 14; matrix products, arithmetic and copies ran while one was open for 24% -> 24% of each run, Pallas kernels for 0% -> 0%
where the time goes in v1:
time: 1180 us; the launch traced here: 1170 us
  waiting for transfers between devices  529 us (45%)
  blocking collectives  218 us (18%)
  matrix products  188 us (16%)
  local copies, waits for them, and re-layouts  119 us (10%)
  other arithmetic  83.4 us (7%)
  between operations  18 us (2%)
  loops' own time  16 us (1%)
    unnamed x21, waiting for transfers between devices  131 us
    reduce_scatter x1, waiting for transfers between devices, body(): lax.psum_scatter(grad_up, 'dp', scatter_dimension=0, tiled=True)  73.3 us
    reduce_scatter x1, waiting for transfers between devices, body(): lax.psum_scatter(grad_down, 'dp', scatter_dimension=1, tiled=True)  72.9 us
    reduce_scatter x1, waiting for transfers between devices, body(): lax.psum_scatter(grad_proj, 'dp', scatter_dimension=0, tiled=True)  63.5 us
    ppermute x2, waiting for transfers between devices, body(): lax.ppermute(line, 'tensor', [(d, (d - have) % ways) for d in range(ways)])  44.4 us
    reduce_scatter x1, waiting for transfers between devices, body(): lax.psum_scatter(times_transposed(dpre_low, up_weight).astype(jnp.bfloat1...  39.1 us
    reduce_scatter x1, waiting for transfers between devices, body(): lax.psum_scatter((through + jnp.take(resid_full, slot_order, axis=0)).ast...  37.3 us
    unnamed x1, blocking collectives  37.3 us
  transfers between devices with their start and end apart: 19, of which 14 were waited for; matrix products, arithmetic and copies ran while one was open for 24% of the time, Pallas kernels for 0%

profile of v1, /device:TPU:0, one launch (start us, length us, event | category | flops | bytes accessed | tf_op | source)
XLA Modules:
  0.0 1174.4 jit_solution(6358301920727628544)
XLA Ops:
  9.5 27.9 %all-gather = bf16[8,96,6]{1,2,0:T(8,128)(2,1)S(1)} all-gather(bf16[1,96,6]{1,2,0:T(8,128)(2,1)S(1)} %convert_bitcast_fusion), channel_id=1, replica_groups=mesh['dp'=8,'tensor'=4] {'dp'}, dimensions={0}, use_global_device_ids=true | all-gather | bytes 10368 | tf_op jit(solution)/shard_map/all_gather | solution.py:149
  39.6 36.3 %all_gather.34 = bf16[3,768,192]{2,0,1:T(4,128)(2,1)S(1)} all-gather(bf16[3,96,192]{2,0,1:T(4,128)(2,1)S(1)} %copy.61), channel_id=1, replica_groups=mesh['dp'=8,'tensor'=4] {'dp'}, dimensions={1}, use_global_device_ids=true | all-gather | bytes 995328 | tf_op jit(solution)/shard_map/all_gather | solution.py:143
  77.0 8.0 scatter_custom_fusion
  85.7 31.2 %all_gather.36 = bf16[192,768]{0,1:T(8,128)(2,1)S(1)} all-gather(bf16[192,96]{0,1:T(8,128)(2,1)S(1)} %copy.66), channel_id=1, replica_groups=mesh['dp'=8,'tensor'=4] {'dp'}, dimensions={1}, use_global_device_ids=true | all-gather | bytes 331776 | tf_op jit(solution)/shard_map/all_gather | solution.py:144
  117.1 12.4 %gather_fusion = bf16[2048,768]{1,0:T(8,128)(2,1)} fusion(bf16[2048,768]{1,0:T(8,128)(2,1)} %all-gather.9.cloned.1.call-done, s32[2048]{0:T(1024)S(1)} %fusion.71), kind=kCustom, calls=%fused_computation | custom fusion | bytes 6299648 | tf_op jit(solution)/shard_map/jit(_take)/gather | solution.py:170
  135.0 49.4 %while.44 = (s32[]{:T(128)}, bf16[4,512,3,64]{1,3,2,0:T(8,128)(2,1)S(1)}, f32[4,3,512]{2,1,0:T(4,128)}, s32[4]{0:T(128)S(1)}, bf16[1,4,512,3,64]{2,4,3,1,0:T(8,1...) while((s32[]{:T(128)}, ...), condition=%wide.region_4.5_spmd.clone, body=%wide.region_1.4_spmd.clone.sunk | while | flops 843055616 | bytes 39975208 | solution.py:60
  140.2 2.8 fusion.140
  143.0 3.7 fusion.141
  155.4 3.7 fusion.141
  167.7 3.7 fusion.141
  180.0 3.7 fusion.141
  189.6 18.1 %all-gather.1 = bf16[8,96,2]{1,2,0:T(2,128)(2,1)S(1)} all-gather(bf16[1,96,2]{1,2,0:T(2,128)(2,1)S(1)} %convert_bitcast_fusion.1), channel_id=1, replica_groups=mesh['dp'=8,'tensor'=4] {'dp'}, dimensions={0}, use_global_device_ids=true | all-gather | bytes 3456 | tf_op jit(solution)/shard_map/all_gather | solution.py:148
  207.8 16.2 %reduce-scatter.20.cloned.1.call-done = bf16[512,768]{1,0:T(8,128)(2,1)} async-done(((bf16[2048,768]{1,0:T(8,128)(2,1)}), bf16[512,768]{1,0:T(8,128)(2,1)}) %reduce-scatter.20.cloned.1.call-update) | async-done | bytes 786448 | tf_op jit(solution)/shard_map/reduce_scatter | solution.py:188
  231.1 26.3 %all-gather.2 = bf16[8,1,384]{2,1,0:T(2,128)(2,1)S(1)} all-gather(bf16[1,1,384]{2,1,0:T(2,128)(2,1)S(1)} %reshape.272), channel_id=1, replica_groups=mesh['dp'=8,'tensor'=4] {'dp'}, dimensions={0}, use_global_device_ids=true | all-gather | bytes 6912 | tf_op jit(solution)/shard_map/all_gather | solution.py:150
  259.5 19.0 %multiply_convert_fusion.1 = (bf16[2048,768]{1,0:T(8,128)(2,1)}, f32[2048,768]{1,0:T(8,128)}, f32[2048,768]{1,0:T(8,128)}) fusion(f32[768]{0:T(1024)S(1)} %dynamic_slice.75, bf16[2048,768]{1,0:T(8,128)(2,1)} %all-gather.11.cloned.1.call-done, bf16[768,768]{1,0:T(8,128)(2,1)} %all-gather.13.cloned.1.call-done), kind=kOutput, calls=%fused_computation.62 | convolution fusion | flops 2519728128 | bytes 20057088 | tf_op jit(solution)/shard_map/dot_general | solution.py:199
  278.5 25.1 %all-gather.15.cloned.1.call-done = bf16[768,768]{0,1:T(8,128)(2,1)} async-done(((bf16[768,96]{0,1:T(8,128)(2,1)}), bf16[768,768]{0,1:T(8,128)(2,1)}) %all-gather.15.cloned.1.call-update) | async-done | bytes 1179664 | tf_op jit(solution)/shard_map/all_gather | solution.py:146
  303.6 6.5 convolution_convert_fusion.1
  311.2 30.6 %all_gather.42 = bf16[768,128]{1,0:T(8,128)(2,1)S(1)} all-gather(bf16[96,128]{1,0:T(8,128)(2,1)S(1)} %convert_element_type.175), channel_id=1, replica_groups=mesh['dp'=8,'tensor'=4] {'dp'}, dimensions={0}, use_global_device_ids=true | all-gather | bytes 221184 | tf_op jit(solution)/shard_map/all_gather | solution.py:147
  341.8 4.5 reduce-scatter.22.cloned.1.call-done
  354.0 9.5 collective-permute-done
  367.0 34.9 %collective-permute-done.1 = bf16[1024,768]{1,0:T(8,128)(2,1)} collective-permute-done((bf16[1024,768]{1,0:T(8,128)(2,1)}, bf16[1024,768]{1,0:T(8,128)(2,1)}, u32[]{:S(2)}, u32[]{:S(2)}) %collective-permute-start.1) | collective-permute-done | bytes 1572896 | tf_op jit(solution)/shard_map/ppermute | solution.py:230
  409.1 10.1 convert_reduce_fusion
  420.9 4.0 convolution_convert_fusion
  425.0 39.1 %reduce-scatter.24.cloned.1.call-done = bf16[512,768]{1,0:T(8,128)(2,1)} async-done(((bf16[2048,768]{1,0:T(8,128)(2,1)}), bf16[512,768]{1,0:T(8,128)(2,1)}) %reduce-scatter.24.cloned.1.call-update) | async-done | bytes 786448 | tf_op jit(solution)/shard_map/reduce_scatter | solution.py:246
  464.1 3.6 multiply_reduce_fusion.2
  470.6 3.1 broadcast.327
  484.5 19.6 %all-gather.17.cloned.1.call-done = bf16[2048,768]{1,0:T(8,128)(2,1)} async-done(((bf16[512,768]{1,0:T(8,128)(2,1)}), bf16[2048,768]{1,0:T(8,128)(2,1)}) %all-gather.17.cloned.1.call-update) | async-done | bytes 3145744 | tf_op jit(solution)/shard_map/all_gather | solution.py:254
  504.1 4.0 convolution_convert_fusion.3
  508.1 3.0 reshape.230
  514.2 119.8 %while.45 = (s32[]{:T(128)}, f32[2048,3,64]{0,2,1:T(8,128)S(1)}, f32[2048,3,64]{0,2,1:T(8,128)}, bf16[4,512,3,64]{1,3,2,0:T(8,128)(2,1)}, s32[4]{0:T(128)S(1)}, ...) while((s32[]{:T(128)}, f32[2048,3,64]{0,2,1:T(8,128)S(1)}, ...), condition=%wide.region_20.21_spmd.clone, body=%wide.region_18.20_spmd.clone.sunk | while | flops 2062516736 | bytes 129419512 | solution.py:111
  520.9 4.9 fusion.153
  525.8 4.8 multiply_reduce_fusion.10
  530.7 5.0 multiply_convert_fusion.3
  535.6 5.7 fusion.154
  550.3 5.5 fusion.153
  555.9 4.8 multiply_reduce_fusion.10
  560.7 5.0 multiply_convert_fusion.3
  565.7 5.6 fusion.154
  580.4 5.5 fusion.153
  585.9 4.8 multiply_reduce_fusion.10
  590.7 5.0 multiply_convert_fusion.3
  595.7 5.7 fusion.154
  610.4 5.5 fusion.153
  615.9 4.8 multiply_reduce_fusion.10
  620.8 5.0 multiply_convert_fusion.3
  625.8 5.6 fusion.154
  640.3 10.6 all-reduce.1
  652.9 4.1 convolution_bitcast_fusion
  657.0 4.6 fusion.64
  664.4 4.7 reshape.281
  669.2 13.4 %gather_fusion.2 = f32[2048,768]{1,0:T(8,128)} fusion(f32[2048,768]{1,0:T(8,128)} %get-tuple-element.574, s32[2048]{0:T(1024)S(1)} %broadcast_clamp_fusion), kind=kCustom, calls=%fused_computation.2 | custom fusion | bytes 12591104 | tf_op jit(solution)/shard_map/jit(_take)/gather | solution.py:282
  682.6 7.0 copy.72
  689.6 18.9 %gather_fusion.1 = bf16[2048,3,192]{2,1,0:T(4,128)(2,1)} fusion(bf16[3,2048,192]{2,0,1:T(4,128)(2,1)} %copy.72, s32[2048]{0:T(1024)S(1)} %broadcast_clamp_fusion), kind=kCustom, calls=%fused_computation.1 | custom fusion | bytes 4726784 | tf_op jit(solution)/shard_map/jit(_take)/gather | solution.py:279
  708.4 9.7 select_bitcast_fusion
  718.1 6.3 fusion.48
  726.5 6.9 fusion.89
  733.5 7.0 fusion.57
  742.7 37.3 %all-reduce = f32[3072]{0:T(1024)S(1)} all-reduce(bf16[3072]{0:T(1024)(128)(2,1)S(1)} %get-tuple-element.552), channel_id=13, replica_groups=mesh['dp'=8,'tensor'=4] {'dp'}, use_global_device_ids=true, to_apply=%region_41.42.clone | all-reduce | flops 3072 | bytes 18432
  783.5 62.3 %reduce-scatter.36.cloned.1.call-done = f32[96,192]{1,0:T(8,128)} async-done(((f32[768,192]{1,0:T(8,128)}), f32[96,192]{1,0:T(8,128)}) %reduce-scatter.36.cloned.1.call-update) | async-done | bytes 73744
  847.4 68.1 %reduce-scatter.34.cloned.1.call-done = f32[96,576]{1,0:T(8,128)} async-done(((f32[768,576]{1,0:T(8,128)}), f32[96,576]{1,0:T(8,128)}) %reduce-scatter.34.cloned.1.call-update) | async-done | bytes 221200
  917.3 37.3 %reduce-scatter.26.cloned.1.call-done = bf16[512,768]{1,0:T(8,128)(2,1)} async-done(((bf16[2048,768]{1,0:T(8,128)(2,1)}), bf16[512,768]{1,0:T(8,128)(2,1)}) %reduce-scatter.26.cloned.1.call-update) | async-done | bytes 786448 | tf_op jit(solution)/shard_map/reduce_scatter | solution.py:281
  957.0 63.5 %reduce-scatter.32.cloned.1.call-done = f32[96,128]{1,0:T(8,128)} async-done(((f32[768,128]{1,0:T(8,128)}), f32[96,128]{1,0:T(8,128)}) %reduce-scatter.32.cloned.1.call-update) | async-done | bytes 49168 | tf_op jit(solution)/shard_map/reduce_scatter | solution.py:310
  1020.5 73.3 %reduce-scatter.28.cloned.1.call-done = f32[96,768]{1,0:T(8,128)} async-done(((f32[768,768]{1,0:T(8,128)}), f32[96,768]{1,0:T(8,128)}) %reduce-scatter.28.cloned.1.call-update) | async-done | bytes 294928 | tf_op jit(solution)/shard_map/reduce_scatter | solution.py:308
  1093.8 72.9 %reduce-scatter.30.cloned.1.call-done = f32[768,96]{0,1:T(8,128)} async-done(((f32[768,768]{0,1:T(8,128)}), f32[768,96]{0,1:T(8,128)}) %reduce-scatter.30.cloned.1.call-update) | async-done | bytes 294928 | tf_op jit(solution)/shard_map/reduce_scatter | solution.py:309
  (286 shorter events, 138.5 us)
Async XLA Ops:
  8.0 68.9 %copy-start.21 = (s32[1,2048]{1,0:T(1,128)S(1)}, s32[1,2048]{1,0:T(1,128)}, u32[]{:S(2)}) copy-start(s32[1,2048]{1,0:T(1,128)} %param.18) | copy-start | bytes 24580
  8.0 109.0 %all-gather.9.cloned.1.call-start = ((), (), s32[]{:S(2)}) async-start(), calls=%async_computation.11 | async-start | bytes 3932160 | tf_op jit(solution)/shard_map/all_gather | solution.py:164
  8.8 215.3 %reduce-scatter.20.cloned.1.call-start = ((), (), s32[]{:S(2)}) async-start(), calls=%async_computation.12 | async-start | bytes 3932160 | tf_op jit(solution)/shard_map/reduce_scatter | solution.py:188
  76.8 54.8 %copy-start.14 = (bf16[3,768,192]{1,2,0:T(8,128)(2,1)}, bf16[3,768,192]{1,2,0:T(8,128)(2,1)S(1)}, u32[]{:S(2)}) copy-start(bf16[3,768,192]{1,2,0:T(8,128)(2,1)S(1)} %copy.62) | copy-start | bytes 2654212
  76.9 52.5 %copy-start.23 = (s32[2048,1]{0,1:T(1,128)}, s32[2048,1]{0,1:T(1,128)S(1)}, u32[]{:S(2)}) copy-start(s32[2048,1]{0,1:T(1,128)S(1)} %compare_select_fusion) | copy-start | bytes 24580
  131.6 2.1 copy-start.4
  184.3 3.6 copy-start.5
  185.1 2.8 copy-start.9
  185.1 4.5 copy-start.42
  187.9 69.6 %all-gather.13.cloned.1.call-start = ((), (), s32[]{:S(2)}) async-start(), calls=%async_computation.14 | async-start | bytes 1327104 | tf_op jit(solution)/shard_map/all_gather | solution.py:145
  189.6 69.9 %all-gather.11.cloned.1.call-start = ((), (), s32[]{:S(2)}) async-start(), calls=%async_computation.13 | async-start | bytes 3932160 | tf_op jit(solution)/shard_map/all_gather | solution.py:197
  224.1 3.6 copy-start.1
  224.1 6.2 copy-start.17
  224.1 7.0 copy-start.39
  227.7 3.4 copy-start.28
  230.2 73.3 %all-gather.15.cloned.1.call-start = ((), (), s32[]{:S(2)}) async-start(), calls=%async_computation.15 | async-start | bytes 1327104 | tf_op jit(solution)/shard_map/all_gather | solution.py:146
  231.0 115.3 %reduce-scatter.22.cloned.1.call-start = ((), (), s32[]{:S(2)}) async-start(), calls=%async_computation.16 | async-start | bytes 3932160 | tf_op jit(solution)/shard_map/reduce_scatter | solution.py:201
  257.5 21.0 %copy-start.37 = (f32[768]{0:T(1024)}, f32[768]{0:T(1024)S(1)}, u32[]{:S(2)}) copy-start(f32[768]{0:T(1024)S(1)} %dynamic_slice.75) | copy-start | bytes 9220
  310.1 36.2 %copy-start.20 = (f32[768]{0:T(1024)S(1)}, f32[768]{0:T(1024)}, u32[]{:S(2)}) copy-start(f32[768]{0:T(1024)} %get-tuple-element.508) | copy-start | bytes 9220
  310.1 36.2 %copy-start.30 = (f32[768]{0:T(1024)S(1)}, f32[768]{0:T(1024)}, u32[]{:S(2)}) copy-start(f32[768]{0:T(1024)} %get-tuple-element.507) | copy-start | bytes 9220
  310.1 38.7 %copy-start.29 = (f32[768]{0:T(1024)S(1)}, f32[768]{0:T(1024)}, u32[]{:S(2)}) copy-start(f32[768]{0:T(1024)} %get-tuple-element.506) | copy-start | bytes 9220
  310.2 153.9 %reduce-scatter.24.cloned.1.call-start = ((), (), s32[]{:S(2)}) async-start(), calls=%async_computation.17 | async-start | bytes 3932160 | tf_op jit(solution)/shard_map/reduce_scatter | solution.py:246
  349.2 2.5 copy-start.6
  350.4 2.0 copy-start.12
  352.4 12.4 %copy-start.2 = (f32[512,768]{1,0:T(8,128)}, f32[512,768]{1,0:T(8,128)S(1)}, u32[]{:S(2)}) copy-start(f32[512,768]{1,0:T(8,128)S(1)} %get-tuple-element.560) | copy-start | bytes 4718596
  352.4 12.4 %copy-start.25 = (f32[512]{0:T(512)}, f32[512]{0:T(512)S(1)}, u32[]{:S(2)}) copy-start(f32[512]{0:T(512)S(1)} %negate_multiply_fusion.2) | copy-start | bytes 6148
  353.6 9.9 copy-start.7
  353.7 9.9 collective-permute-start
  364.8 37.1 %collective-permute-start.1 = (bf16[1024,768]{1,0:T(8,128)(2,1)}, bf16[1024,768]{1,0:T(8,128)(2,1)}, u32[]{:S(2)}, u32[]{:S(2)}) collective-permute-start(bf16[1024,768]{1,0:T(8,128)(2,1)} %pad_maximum_fusion.1), channel_id=1, source_target_pairs={{0,2},{1,3},{2,0},{3,1},{4,6},{5,7},{6,4},{7,5},{8,10},{9,11},{10,... | collective-permute-start | bytes 4718600 | tf_op jit(solution)/shard_map/ppermute | solution.py:230
  366.0 38.5 %copy-start.8 = (bf16[512,768]{1,0:T(8,128)(2,1)S(1)}, bf16[512,768]{1,0:T(8,128)(2,1)}, u32[]{:S(2)}) copy-start(bf16[512,768]{1,0:T(8,128)(2,1)} %copy-done.7) | copy-start | bytes 2359300
  404.5 4.6 copy-start.38
  404.5 4.6 copy-start.41
  409.1 11.8 %copy-start.40 = (bf16[768,768]{1,0:T(8,128)(2,1)S(1)}, bf16[768,768]{1,0:T(8,128)(2,1)}, u32[]{:S(2)}) copy-start(bf16[768,768]{1,0:T(8,128)(2,1)} %all-gather.13.cloned.1.call-done) | copy-start | bytes 3538948
  419.2 1.7 copy-start.44
  424.9 79.2 %all-gather.17.cloned.1.call-start = ((), (), s32[]{:S(2)}) async-start(), calls=%async_computation.18 | async-start | bytes 3932160 | tf_op jit(solution)/shard_map/all_gather | solution.py:254
  464.1 4.3 copy-start.3
  464.1 4.3 copy-start.11
  473.7 2.4 copy-start.36
  475.3 249.1 %all-reduce.4.cloned.1.call-start = ((), (), s32[]{:S(2)}) async-start(), calls=%async_computation.22 | async-start | bytes 393216 | tf_op jit(solution)/shard_map/psum | solution.py:300
  478.9 301.6 %reduce-scatter.38.cloned.1.call-start = ((), (), s32[]{:S(2)}) async-start(), calls=%async_computation.26 | async-start | bytes 442368
  480.1 33.2 %copy-start.26 = (bf16[3072]{0:T(1024)(128)(2,1)}, bf16[3072]{0:T(1024)(128)(2,1)S(1)}, u32[]{:S(2)}) copy-start(bf16[3072]{0:T(1024)(128)(2,1)S(1)} %dynamic_update_slice.46) | copy-start | bytes 18436
  535.6 5.7 copy-start
  565.7 5.6 copy-start
  595.7 5.7 copy-start
  625.8 5.6 copy-start
  636.4 3.7 copy-start.32
  636.4 3.7 copy-start.33
  636.4 3.7 copy-start.34
  636.4 3.7 copy-start.35
  636.5 3.8 copy-start.27
  636.5 3.8 copy-start.31
  638.0 14.9 %copy-start.10 = (bf16[24,8,4,512]{3,1,2,0:T(8,128)(2,1)S(1)}, bf16[24,8,4,512]{3,1,2,0:T(8,128)(2,1)}, u32[]{:S(2)}) copy-start(bf16[24,8,4,512]{3,1,2,0:T(8,128)(2,1)} %copy-done.9) | copy-start | bytes 2359300
  651.8 130.2 %reduce-scatter.40.cloned.1.call-start = ((), (), s32[]{:S(2)}) async-start(), calls=%async_computation.27 | async-start | bytes 442368
  652.8 192.9 %reduce-scatter.36.cloned.1.call-start = ((), (), s32[]{:S(2)}) async-start(), calls=%async_computation.25 | async-start | bytes 884736
  657.0 258.5 %reduce-scatter.34.cloned.1.call-start = ((), (), s32[]{:S(2)}) async-start(), calls=%async_computation.24 | async-start | bytes 2211840
  664.4 4.8 copy-start.22
  664.4 4.8 copy-start.24
  669.1 285.5 %reduce-scatter.26.cloned.1.call-start = ((), (), s32[]{:S(2)}) async-start(), calls=%async_computation.19 | async-start | bytes 3932160 | tf_op jit(solution)/shard_map/reduce_scatter | solution.py:281
  708.4 9.7 copy-start.15
  724.4 296.1 %reduce-scatter.32.cloned.1.call-start = ((), (), s32[]{:S(2)}) async-start(), calls=%async_computation.23 | async-start | bytes 442368 | tf_op jit(solution)/shard_map/reduce_scatter | solution.py:310
  726.2 367.6 %reduce-scatter.28.cloned.1.call-start = ((), (), s32[]{:S(2)}) async-start(), calls=%async_computation.20 | async-start | bytes 2654208 | tf_op jit(solution)/shard_map/reduce_scatter | solution.py:308
  733.5 7.1 copy-start.43
  733.5 8.3 copy-start.13
  733.5 433.3 %reduce-scatter.30.cloned.1.call-start = ((), (), s32[]{:S(2)}) async-start(), calls=%async_computation.21 | async-start | bytes 2654208 | tf_op jit(solution)/shard_map/reduce_scatter | solution.py:309
  (3 other events, 2.7 us)
Sparse Core Ops, SparseCore 0:
  10.4 31.2 all-gather.8
  188.0 35.9 reduce-scatter.19
  425.1 38.9 reduce-scatter.23
  479.1 47.6 all-reduce.3
Sparse Core Ops, SparseCore 1:
  191.2 39.5 all-gather.12
  232.7 26.7 all-gather.10
  262.1 41.4 all-gather.14
  310.2 36.1 reduce-scatter.21
  475.4 28.6 all-gather.16
  651.9 63.3 reduce-scatter.37
  718.4 61.1 reduce-scatter.39
  783.4 62.3 reduce-scatter.35
  849.1 66.3 reduce-scatter.33
  918.0 36.6 reduce-scatter.25
  958.3 62.2 reduce-scatter.31
  1024.6 69.1 reduce-scatter.27
  1097.8 68.9 reduce-scatter.29
